TPU v7x, 32 devices: a whole 2x2x4 slice. The times are simulated.
32 devices in a mesh: dp: 2 (over z_hi), expert: 8 (over y, x, core), tensor: 2 (over z_lo).
Axes of the slice: x: 2, y: 2, z: 4 (z_hi: 2, z_lo: 2; z = z_hi * 2 + z_lo), core: 2. Of those that a mesh axis runs over, the one named last changes fastest.
Arguments:
- tokens: bfloat16 [2048, 2048], P(('dp', 'expert')), may hold values from -6 to 6
- expert_ids: int32 [2048, 8], P(('dp', 'expert')), may hold values from 0 to 15, all different within a row; in each aligned block of 64 rows (0 to 63, 64 to 127, ...) at most 64 rows name the same one
- weights: bfloat16 [2, 16, 768, 2048], P(None, 'expert', 'tensor'), may hold values from -0.125 to 0.125
- first_moment: bfloat16 [2, 16, 768, 2048], P('dp', 'expert', 'tensor'), may hold values from -6 to 6
- second_moment: bfloat16 [2, 16, 768, 2048], P('dp', 'expert', 'tensor'), may hold values from 1 to 100
- hidden_grad: bfloat16 [2, 16, 768, 1024], P('dp', 'expert', 'tensor'), may hold values from -6 to 6
- swap_list: int32 [4, 2], replicated, may hold values from 0 to 15, as said below
Outputs:
- hidden: bfloat16 [2, 16, 768, 1024], P('dp', 'expert', 'tensor')
- token_grad: bfloat16 [2048, 2048], P(('dp', 'expert', 'tensor'))
- new_weights: bfloat16 [2, 16, 768, 2048], P('dp', 'expert', 'tensor')
- new_first: bfloat16 [2, 16, 768, 2048], P('dp', 'expert', 'tensor')
- new_second: bfloat16 [2, 16, 768, 2048], P('dp', 'expert', 'tensor')
Inputs may be any that keep to these rules, and one draw needn't show every extreme that they name: `expert_ids`: each row names 8 different experts. Within the rows of one quarter block of 64 rows no expert is named by more than 64 rows, a bound that some block reaches. `swap_list`: expert e is owned by index e // 2 of expert. The owners of the two experts of a row are 4 indices apart, and no owner appears in two rows.
All inputs are finite; a program needn't handle non-finite values.
Results may differ from a plain program's by a relative error of at most 0.0065.
Values may be sent and summed in bfloat16 or wider, within the bound.
No kernel may reach another device: no remote copies, remote signals or barrier semaphores. Data moves between devices by JAX's collectives and lax.ppermute only.
A program may use at most 192 MiB of HBM per device.

v0:
```python
import jax
import jax.numpy as jnp
from jax import lax
from jax.sharding import PartitionSpec as P

beta_one = 0.9
beta_two = 0.95
step_size = 0.01
adam_eps = 1e-08


def partner(value, axis, bit):
    return lax.ppermute(value, axis, [(i, i ^ 1 << bit) for i in range(lax.axis_size(axis))])


def slot_select(expert_ids, blocks, per_dev, owners, capacity):
    row_total = expert_ids.shape[0]
    top_count = expert_ids.shape[1]
    pair_total = row_total * top_count
    block_pairs = pair_total // blocks
    expert_total = per_dev * owners
    named_flat = expert_ids.reshape(blocks, block_pairs)
    one_hot = (
        named_flat[:, :, None] == jnp.arange(expert_total, dtype=jnp.int32)[None, None, :]
    ).astype(jnp.int32)
    slot_rank = (jnp.sum(jnp.cumsum(one_hot, axis=1) * one_hot, axis=2) - 1).reshape(pair_total)
    block_index = jnp.arange(pair_total, dtype=jnp.int32) // block_pairs
    expert_flat = named_flat.reshape(pair_total)
    slot_key = (
        (expert_flat % per_dev * owners + expert_flat // per_dev) * blocks + block_index
    ) * capacity + slot_rank
    key_total = expert_total * blocks * capacity
    by_key = (jnp.arange(key_total, dtype=jnp.int32)[:, None] == slot_key[None, :]).astype(
        jnp.bfloat16
    )
    pair_rows = jnp.arange(pair_total, dtype=jnp.int32) // top_count
    by_row = (pair_rows[:, None] == jnp.arange(row_total, dtype=jnp.int32)[None, :]).astype(
        jnp.bfloat16
    )
    return jnp.dot(by_key, by_row, preferred_element_type=jnp.float32).astype(jnp.bfloat16)


def migration_slot(swap_list, per_dev):
    own_index = lax.axis_index("expert")
    first_hit = swap_list[:, 0] // per_dev == own_index
    second_hit = swap_list[:, 1] // per_dev == own_index
    chosen = jnp.sum(
        jnp.where(first_hit, swap_list[:, 0] % per_dev, 0)
        + jnp.where(second_hit, swap_list[:, 1] % per_dev, 0)
    )
    return (chosen, jnp.any(first_hit | second_hit))


def pick_slot(state, chosen):
    return lax.dynamic_index_in_dim(state, chosen, 1, keepdims=False)


def place_slot(state, incoming, chosen, moving):
    target = (jnp.arange(state.shape[1], dtype=jnp.int32) == chosen) & moving
    return jnp.where(target[None, :, None, None], incoming[:, None], state)


def adam_step(weight_half, first_moment, second_moment, weight_grad):
    first_next = beta_one * first_moment.astype(jnp.float32) + (1.0 - beta_one) * weight_grad
    second_next = (
        beta_two * second_moment.astype(jnp.float32) + (1.0 - beta_two) * weight_grad * weight_grad
    )
    updated = weight_half.astype(jnp.float32) - step_size * first_next / (
        jnp.sqrt(second_next) + adam_eps
    )
    return (
        updated.astype(jnp.bfloat16),
        first_next.astype(jnp.bfloat16),
        second_next.astype(jnp.bfloat16),
    )


def shards(tokens, expert_ids, weights, first_moment, second_moment, hidden_grad, swap_list):
    owners = lax.axis_size("expert")
    tensor_count = lax.axis_size("tensor")
    replicas = lax.axis_size("dp")
    per_dev = weights.shape[1]
    model_width = tokens.shape[1]
    slots_total = hidden_grad.shape[3]
    capacity = slots_total // (owners * tensor_count)
    quarter_rows = tokens.shape[0] // tensor_count
    quarter_index = lax.axis_index("tensor")
    whole_select = slot_select(expert_ids, tensor_count, per_dev, owners, capacity)
    outgoing = jnp.dot(whole_select, tokens, preferred_element_type=jnp.float32).astype(
        jnp.bfloat16
    )
    outgoing = outgoing.reshape(per_dev, owners, tensor_count * capacity, model_width)
    arrived = lax.all_to_all(outgoing, "expert", split_axis=1, concat_axis=1, tiled=True)
    select_grid = whole_select.reshape(
        per_dev, owners, tensor_count, capacity, tensor_count, quarter_rows
    )
    select_grid = lax.dynamic_index_in_dim(select_grid, quarter_index, 2, keepdims=False)
    select_grid = lax.dynamic_index_in_dim(select_grid, quarter_index, 3, keepdims=False)
    own_select = select_grid.reshape(per_dev * owners * capacity, quarter_rows)
    routed = arrived.reshape(per_dev, slots_total, model_width)
    half_rows = 2 // replicas
    replica_index = lax.axis_index("dp")
    weight_half = lax.dynamic_slice_in_dim(weights, replica_index * half_rows, half_rows, 0)
    chosen, moving = migration_slot(swap_list, per_dev)
    top_bit = owners.bit_length() - 2
    projected = jnp.einsum("cefd,esd->ecfs", weights, routed, preferred_element_type=jnp.float32)
    gate_pre = projected[:, 0]
    up_pre = projected[:, 1]
    sigmoid_gate = jax.nn.sigmoid(gate_pre)
    hidden = (gate_pre * sigmoid_gate * up_pre).astype(jnp.bfloat16)
    grad_hidden = hidden_grad[0].astype(jnp.float32)
    grad_gate = grad_hidden * up_pre * sigmoid_gate * (1.0 + gate_pre * (1.0 - sigmoid_gate))
    grad_up = grad_hidden * gate_pre * sigmoid_gate
    grad_pre = jnp.stack([grad_gate, grad_up], axis=1).astype(jnp.bfloat16)
    slot_terms = jnp.einsum("ecfs,cefd->esd", grad_pre, weights, preferred_element_type=jnp.float32)
    slot_terms = slot_terms.reshape(per_dev, owners, tensor_count, capacity, model_width)
    summed = lax.psum_scatter(
        slot_terms.astype(jnp.bfloat16), "tensor", scatter_dimension=2, tiled=True
    )
    returning = summed.reshape(per_dev, owners, capacity, model_width)
    back_rows = lax.all_to_all(returning, "expert", split_axis=1, concat_axis=1, tiled=True)
    token_grad = jnp.dot(
        own_select.T,
        back_rows.reshape(per_dev * owners * capacity, model_width),
        preferred_element_type=jnp.float32,
    ).astype(jnp.bfloat16)

    def grad_rows(offset, number):
        part_grad = lax.dynamic_slice_in_dim(grad_pre, offset, number, 1)
        return jnp.einsum("esd,ecfs->cefd", routed, part_grad, preferred_element_type=jnp.float32)

    own_term = grad_rows(replica_index * half_rows, half_rows)
    other_term = grad_rows((1 - replica_index) * half_rows, half_rows)
    weight_grad = own_term + partner(other_term, "dp", 0)
    updated, first_next, second_next = adam_step(
        weight_half, first_moment, second_moment, weight_grad
    )
    arrived_states = partner(
        (pick_slot(updated, chosen), pick_slot(first_next, chosen), pick_slot(second_next, chosen)),
        "expert",
        top_bit,
    )
    new_weights = place_slot(updated, arrived_states[0], chosen, moving)
    new_first = place_slot(first_next, arrived_states[1], chosen, moving)
    new_second = place_slot(second_next, arrived_states[2], chosen, moving)
    return (hidden[None], token_grad, new_weights, new_first, new_second)


def solution(mesh):
    in_specs = (
        P(("dp", "expert"), None),
        P(("dp", "expert"), None),
        P(None, "expert", "tensor", None),
        P("dp", "expert", "tensor", None),
        P("dp", "expert", "tensor", None),
        P("dp", "expert", "tensor", None),
        P(),
    )
    out_specs = (
        P("dp", "expert", "tensor", None),
        P(("dp", "expert", "tensor"), None),
        P("dp", "expert", "tensor", None),
        P("dp", "expert", "tensor", None),
        P("dp", "expert", "tensor", None),
    )
    return jax.shard_map(shards, mesh=mesh, in_specs=in_specs, out_specs=out_specs, check_vma=False)
```

profile of v0, /device:TPU:27, one launch (start us, length us, event | category | flops | bytes accessed | tf_op | source)
XLA Modules:
  0.0 668.8 jit_solution(12819132871745916266)
XLA Ops:
  8.3 2.3 reduce-window.6
  11.1 1.6 fusion.20
  12.8 5.6 convolution_convert_fusion
  18.3 8.3 %copy.45 = bf16[2,8,128,2048]{3,2,0,1:T(8,128)(2,1)} copy(bf16[2,8,128,2048]{3,2,1,0:T(8,128)(2,1)} %bitcast.124) | data formatting | bytes 16777216 | tf_op jit(solution)/shard_map/reshape | solution.py:92
  26.6 5.7 all-to-all-start
  32.4 1.9 copy.49
  34.2 90.7 %all-to-all-done = bf16[2,8,128,2048]{3,2,0,1:T(8,128)(2,1)} async-done(((bf16[2,8,128,2048]{3,2,0,1:T(8,128)(2,1)}), bf16[2,8,128,2048]{3,2,0,1:T(8,128)(2,1)}, u32[]{:S(2)}, u32[]{:S(2)}) %all-to-all-start) | async-done | bytes 8388640 | tf_op jit(solution)/shard_map/all_to_all | solution.py:93
  124.9 8.4 %copy.46 = bf16[2,8,128,2048]{3,2,1,0:T(8,128)(2,1)} copy(bf16[2,8,128,2048]{3,2,0,1:T(8,128)(2,1)} %all-to-all-done) | data formatting | bytes 16777216 | tf_op jit(solution)/shard_map/all_to_all | solution.py:93
  133.3 10.2 %fusion.17 = f32[2,2,384,1024]{2,3,1,0:T(8,128)S(1)} fusion(bf16[2,1024,2048,1]{2,1,3,0:T(8,128)(2,1)} %bitcast.126, bf16[2,2,384,2048]{3,2,1,0:T(8,128)(2,1)} %param.9), kind=kOutput, calls=%fused_computation.40 | convolution fusion | flops 6442450944 | bytes 20971520 | tf_op jit(solution)/shard_map/cefd,esd->ecfs/dot_general | solution.py:106
  143.6 1.6 fusion.10
  146.3 8.9 %bitcast_convert_fusion = bf16[2,1024,2048]{2,1,0:T(8,128)(2,1)} fusion(bf16[2,2,384,2048]{3,2,1,0:T(8,128)(2,1)S(1)} %bitcast.133, bf16[2,1,384,1024]{2,3,1,0:T(8,128)(2,1)S(1)} %get-tuple-element.32, bf16[2,1,384,1024]{2,3,1,0:T(8,128)(2,1)S(1)} %get-tuple-element.31), kind=kOutput, calls=%fused_computation | convolution fusion | flops 6448218112 | bytes 17825792 | tf_op jit(solution)/shard_map/ecfs,cefd->esd/dot_general | solution.py:115
  156.6 9.6 %convolution_bitcast_fusion = f32[1,2,384,2048]{3,2,1,0:T(8,128)} fusion(bf16[2,1024,2048]{2,1,0:T(8,128)(2,1)} %bitcast.127, s32[]{:T(128)S(6)} %select_n.103, bf16[2,1,384,1024]{2,3,1,0:T(8,128)(2,1)S(1)} %copy-done.7, bf16[2,1,384,1024]{2,3,1,0:T(8,128)(2,1)} %copy-done.8), kind=kOutput, calls=%fused_computation.21 | convolution fusion | flops 3222011904 | bytes 17825796 | tf_op jit(solution)/shard_map/esd,ecfs->cefd/dot_general | solution.py:130
  170.0 321.0 %all-reduce.3.cloned.1.call-done = bf16[2,8,2,64,2048]{4,3,2,1,0:T(8,128)(2,1)} async-done(((bf16[2,8,2,64,2048]{4,3,2,1,0:T(8,128)(2,1)}), bf16[2,8,2,64,2048]{4,3,2,1,0:T(8,128)(2,1)}) %all-reduce.3.cloned.1.call-update) | async-done | bytes 8388624
  491.0 3.1 dynamic-slice_bitcast_fusion
  494.1 2.2 copy.51
  496.4 4.7 all-to-all-start.1
  501.1 14.5 %fusion.7 = (bf16[1,2,384,2048]{3,2,1,0:T(8,128)(2,1)S(1)}, bf16[1,2,384,2048]{3,2,1,0:T(8,128)(2,1)S(1)}, bf16[1,2,384,2048]{3,2,1,0:T(8,128)(2,1)}) fusion(bf16[1,2,384,2048]{3,2,1,0:T(8,128)(2,1)} %param.11, bf16[1,2,384,2048]{3,2,1,0:T(8,128)(2,1)} %param.10, bf16[2,2,384,2048]{3,2,1,0:T(8,128)(2,1)} %param.9, s32[]{:T(128)S(6)} %select_n.102, ...), kind=kOutput, calls=%fused_computation.23 | convolution fusion | flops 3250323456 | bytes 36701184 | tf_op jit(solution)/shard_map/esd,ecfs->cefd/dot_general | solution.py:130
  525.6 3.7 fusion.13
  529.3 1.6 copy.55
  530.9 50.3 %collective-permute-done.2 = bf16[1,384,2048]{2,1,0:T(8,128)(2,1)} collective-permute-done((bf16[1,384,2048]{2,1,0:T(8,128)(2,1)}, bf16[1,384,2048]{2,1,0:T(8,128)(2,1)}, u32[]{:S(2)}, u32[]{:S(2)}) %collective-permute-start.2) | collective-permute-done | bytes 1572896 | tf_op jit(solution)/shard_map/ppermute | solution.py:13
  581.3 33.7 %collective-permute-done.1 = bf16[1,384,2048]{2,1,0:T(8,128)(2,1)} collective-permute-done((bf16[1,384,2048]{2,1,0:T(8,128)(2,1)}, bf16[1,384,2048]{2,1,0:T(8,128)(2,1)}, u32[]{:S(2)}, u32[]{:S(2)}) %collective-permute-start.1) | collective-permute-done | bytes 1572896 | tf_op jit(solution)/shard_map/ppermute | solution.py:13
  615.0 33.7 %collective-permute-done.3 = bf16[1,384,2048]{2,1,0:T(8,128)(2,1)} collective-permute-done((bf16[1,384,2048]{2,1,0:T(8,128)(2,1)}, bf16[1,384,2048]{2,1,0:T(8,128)(2,1)}, u32[]{:S(2)}, u32[]{:S(2)}) %collective-permute-start.3) | collective-permute-done | bytes 1572896 | tf_op jit(solution)/shard_map/ppermute | solution.py:13
  648.7 9.1 %broadcast_select_fusion = (bf16[1,2,384,2048]{3,2,1,0:T(8,128)(2,1)}, bf16[1,2,384,2048]{3,2,1,0:T(8,128)(2,1)}, bf16[1,2,384,2048]{3,2,1,0:T(8,128)(2,1)}) fusion(bf16[1,2,384,2048]{3,2,1,0:T(8,128)(2,1)} %copy-done.3, pred[2]{0:T(512)(128)(4,1)S(1)} %compare_and_fusion, bf16[384,2048]{1,0:T(8,128)(2,1)} %bitcast.26, ...), kind=kLoop, calls=%fused_computation.37 | loop fusion | flops 4718592 | bytes 23592962 | tf_op jit(solution)/shard_map/jit(_where)/select_n | solution.py:60
  657.8 2.6 copy.52
  (58 shorter events, 17.4 us)
Async XLA Ops:
  7.2 5.6 copy-start
  26.6 98.3 %all-to-all-start = ((bf16[2,8,128,2048]{3,2,0,1:T(8,128)(2,1)}), bf16[2,8,128,2048]{3,2,0,1:T(8,128)(2,1)}, u32[]{:S(2)}, u32[]{:S(2)}) async-start(bf16[2,8,128,2048]{3,2,0,1:T(8,128)(2,1)} %copy.45), calls=%async_computation | async-start | bytes 16777216 | tf_op jit(solution)/shard_map/all_to_all | solution.py:93
  32.3 458.6 %all-reduce.3.cloned.1.call-start = ((), (), s32[]{:S(2)}) async-start(), calls=%async_computation.2 | async-start | bytes 16777216
  124.9 21.4 %slice-start = ((s8[6291456]{0:T(1024)(128)(4,1)}), s8[2097152]{0:T(1024)(128)(4,1)S(1)}, s32[]{:S(2)}) async-start(s8[6291456]{0:T(1024)(128)(4,1)} %bitcast.132), calls=%async_computation.3 | async-start | bytes 4194304
  133.3 12.9 %slice-start.1 = ((s8[6291456]{0:T(1024)(128)(4,1)}), s8[4194304]{0:T(1024)(128)(4,1)S(1)}, s32[]{:S(2)}) async-start(s8[6291456]{0:T(1024)(128)(4,1)} %bitcast.132), calls=%async_computation.4 | async-start | bytes 8388608
  143.6 2.7 copy-start.2
  146.3 8.9 %copy-start.6 = (bf16[2,1,384,1024]{2,3,1,0:T(8,128)(2,1)}, bf16[2,1,384,1024]{2,3,1,0:T(8,128)(2,1)S(1)}, u32[]{:S(2)}) copy-start(bf16[2,1,384,1024]{2,3,1,0:T(8,128)(2,1)S(1)} %get-tuple-element.31) | copy-start | bytes 4718596
  146.3 8.9 %copy-start.8 = (bf16[2,1,384,1024]{2,3,1,0:T(8,128)(2,1)}, bf16[2,1,384,1024]{2,3,1,0:T(8,128)(2,1)S(1)}, u32[]{:S(2)}) copy-start(bf16[2,1,384,1024]{2,3,1,0:T(8,128)(2,1)S(1)} %get-tuple-element.32) | copy-start | bytes 4718596
  155.2 1.4 copy-start.7
  156.6 10.1 %copy-start.9 = (s32[4,2]{0,1:T(2,128)S(1)}, s32[4,2]{0,1:T(2,128)}, u32[]{:S(2)}) copy-start(s32[4,2]{0,1:T(2,128)} %param.13) | copy-start | bytes 100
  156.6 12.1 %copy-start.10 = (u32[32]{0:T(128)S(1)}, u32[32]{0:T(128)}, u32[]{:S(2)}) copy-start(u32[32]{0:T(128)} %constant.173) | copy-start | bytes 388
  166.2 334.9 %collective-permute-start = (f32[1,2,384,2048]{3,2,1,0:T(8,128)}, f32[1,2,384,2048]{3,2,1,0:T(8,128)}, u32[]{:S(2)}, u32[]{:S(2)}) collective-permute-start(f32[1,2,384,2048]{3,2,1,0:T(8,128)} %convolution_bitcast_fusion), channel_id=1, source_target_pairs={{0,16},{16,0},{1,17},{17,1},{2,18},{18,2},{3,19},{19,3},{4,20},{20... | collective-permute-start | bytes 18874376 | tf_op jit(solution)/shard_map/ppermute | solution.py:13
  496.4 161.5 %all-to-all-start.1 = ((bf16[2,8,64,2048]{3,2,0,1:T(8,128)(2,1)}), bf16[2,8,64,2048]{3,2,0,1:T(8,128)(2,1)}, u32[]{:S(2)}, u32[]{:S(2)}) async-start(bf16[2,8,64,2048]{3,2,0,1:T(8,128)(2,1)} %copy.51), calls=%async_computation.1 | async-start | bytes 8388608 | tf_op jit(solution)/shard_map/all_to_all | solution.py:121
  515.6 3.1 copy-start.3
  515.6 4.2 copy-start.4
  515.6 4.2 copy-start.5
  521.0 60.3 %collective-permute-start.2 = (bf16[1,384,2048]{2,1,0:T(8,128)(2,1)}, bf16[1,384,2048]{2,1,0:T(8,128)(2,1)}, u32[]{:S(2)}, u32[]{:S(2)}) collective-permute-start(bf16[1,384,2048]{2,1,0:T(8,128)(2,1)} %dynamic-slice_bitcast_fusion.2), channel_id=1, source_target_pairs={{0,8},{2,10},{4,12},{6,14},{8,0},{10,2},{12,4},{14,6},{1,9},{3,11}... | collective-permute-start | bytes 4718600 | tf_op jit(solution)/shard_map/ppermute | solution.py:13
  521.1 93.9 %collective-permute-start.1 = (bf16[1,384,2048]{2,1,0:T(8,128)(2,1)}, bf16[1,384,2048]{2,1,0:T(8,128)(2,1)}, u32[]{:S(2)}, u32[]{:S(2)}) collective-permute-start(bf16[1,384,2048]{2,1,0:T(8,128)(2,1)} %dynamic-slice_bitcast_fusion.3), channel_id=1, source_target_pairs={{0,8},{2,10},{4,12},{6,14},{8,0},{10,2},{12,4},{14,6},{1,9},{3,11}... | collective-permute-start | bytes 4718600 | tf_op jit(solution)/shard_map/ppermute | solution.py:13
  522.5 126.2 %collective-permute-start.3 = (bf16[1,384,2048]{2,1,0:T(8,128)(2,1)}, bf16[1,384,2048]{2,1,0:T(8,128)(2,1)}, u32[]{:S(2)}, u32[]{:S(2)}) collective-permute-start(bf16[1,384,2048]{2,1,0:T(8,128)(2,1)} %dynamic-slice_bitcast_fusion.1), channel_id=1, source_target_pairs={{0,8},{2,10},{4,12},{6,14},{8,0},{10,2},{12,4},{14,6},{1,9},{3,11}... | collective-permute-start | bytes 4718600 | tf_op jit(solution)/shard_map/ppermute | solution.py:13
  657.8 4.2 copy-start.1
Sparse Core Ops, SparseCore 0:
  155.4 335.5 all-reduce.2
where the time goes:
time: 669 us
  waiting for transfers between devices  530 us (79%)
  matrix products  52 us (8%)
  local copies, waits for them, and re-layouts  39.1 us (6%)
  other arithmetic  19.5 us (3%)
  between operations  16.2 us (2%)
  starting transfers between devices  12.6 us (2%)
    unnamed x2, waiting for transfers between devices  321 us
    ppermute x4, waiting for transfers between devices, partner(): lax.ppermute(value, axis, [(i, i ^ 1 << bit) for i in range(lax.axis_size...  118 us
    all_to_all x1, waiting for transfers between devices, shards(): lax.all_to_all(outgoing, 'expert', split_axis=1, concat_axis=1, tiled=True)  90.7 us
    dot_general x2, matrix products, grad_rows(): jnp.einsum('esd,ecfs->cefd', routed, part_grad, preferred_element_type=jn...  24.1 us
  transfers between devices with their start and end apart: 7, of which 5 were waited for; matrix products, arithmetic and copies ran while one was open for 8% of the time, Pallas kernels for 0%

commit v1 on v0

--- a/solution.py
+++ b/solution.py
@@ -1,3 +1,4 @@
+import functools
 import jax
 import jax.numpy as jnp
 from jax import lax
@@ -7,6 +8,41 @@
 beta_two = 0.95
 step_size = 0.01
 adam_eps = 1e-08
+
+
+def state_types(array_in, axis_no, body):
+    frame_out = array_in.shape
+    left_arr = array_in.reshape(
+        *frame_out[:axis_no], body, frame_out[axis_no] // body, *frame_out[axis_no + 1 :]
+    )
+    q_next = jnp.moveaxis(left_arr, axis_no, 0)
+    return q_next
+
+
+def meet_slabs_on_mesh(slab_in, d0):
+    y1 = list(slab_in.shape[1:])
+    y1[d0] *= slab_in.shape[0]
+    y2 = jnp.moveaxis(slab_in, 0, d0).reshape(y1)
+    return y2
+
+
+def _settle_spans(view, comm_axis, piece_in, content):
+    arr_now = jax.lax.psum(1, comm_axis)
+    mid_arr = jax.lax.axis_index(comm_axis)
+    arr_out, z2 = (arr_now, mid_arr)
+    long_array = state_types(view, piece_in, arr_out)
+    heap = [long_array[z2]]
+    for src_i in range(1, arr_out):
+        back = long_array[z2 ^ src_i]
+        plain = jax.lax.ppermute(back, comm_axis, [(j, j ^ src_i) for j in range(arr_out)])
+        heap.append(plain)
+    t_next = jnp.stack(heap, axis=0)
+    long_array = t_next[z2 ^ jnp.arange(arr_out)]
+    block_next = meet_slabs_on_mesh(long_array, content)
+    return block_next
+
+
+check_sector = functools.partial(_settle_spans, comm_axis="expert", piece_in=1, content=1)
 
 
 def partner(value, axis, bit):
@@ -90,7 +126,7 @@
         jnp.bfloat16
     )
     outgoing = outgoing.reshape(per_dev, owners, tensor_count * capacity, model_width)
-    arrived = lax.all_to_all(outgoing, "expert", split_axis=1, concat_axis=1, tiled=True)
+    arrived = check_sector(outgoing)
     select_grid = whole_select.reshape(
         per_dev, owners, tensor_count, capacity, tensor_count, quarter_rows
     )

time: 669 us -> 683 us (1.021)
  local copies, waits for them, and re-layouts: 39.1 us -> 60.5 us
  waiting for transfers between devices: 530 us -> 519 us
    all_to_all x1 -> x0, waiting for transfers between devices: 90.7 us -> none  [shards(): lax.all_to_all(outgoing, 'expert', split_axis=1, concat_axis=1, tiled=True)]
    ppermute x0 -> x7, waiting for transfers between devices: none -> 80.7 us  [_settle_spans(): jax.lax.ppermute(back, comm_axis, [(j, j ^ src_i) for j in range(arr_out)])]
    unnamed x32 -> x41, local copies, waits for them, and re-layouts: 8.94 us -> 25 us
    ppermute x0 -> x7, starting transfers between devices: none -> 8.83 us  [_settle_spans(): jax.lax.ppermute(back, comm_axis, [(j, j ^ src_i) for j in range(arr_out)])]
    transpose x0 -> x1, local copies, waits for them, and re-layouts: none -> 8.42 us  [meet_slabs_on_mesh(): y2 = jnp.moveaxis(slab_in, 0, d0).reshape(y1)]
    all_to_all x1 -> x0, local copies, waits for them, and re-layouts: 8.42 us -> none  [shards(): lax.all_to_all(outgoing, 'expert', split_axis=1, concat_axis=1, tiled=True)]
    reshape x1 -> x0, local copies, waits for them, and re-layouts: 8.27 us -> none  [shards(): outgoing.reshape(per_dev, owners, tensor_count * capacity, model_width)]
    gather x0 -> x1, local copies, waits for them, and re-layouts: none -> 8.06 us  [_settle_spans(): long_array = t_next[z2 ^ jnp.arange(arr_out)]]
  transfers between devices with their start and end apart: 7 -> 13, of which waited for: 5 -> 7; matrix products, arithmetic and copies ran while one was open for 8% -> 10% of each run, Pallas kernels for 0% -> 0%
where the time goes in v1:
time: 683 us; the launch traced here: 682 us
  waiting for transfers between devices  519 us (76%)
  local copies, waits for them, and re-layouts  60.5 us (9%)
  matrix products  48.9 us (7%)
  other arithmetic  19.5 us (3%)
  starting transfers between devices  17.6 us (3%)
  between operations  16.3 us (2%)
    unnamed x2, waiting for transfers between devices  321 us
    ppermute x4, waiting for transfers between devices, partner(): lax.ppermute(value, axis, [(i, i ^ 1 << bit) for i in range(lax.axis_size...  118 us
    ppermute x7, waiting for transfers between devices, _settle_spans(): jax.lax.ppermute(back, comm_axis, [(j, j ^ src_i) for j in range(arr_out)])  80.7 us
    unnamed x41, local copies, waits for them, and re-layouts  25 us
    dot_general x2, matrix products, grad_rows(): jnp.einsum('esd,ecfs->cefd', routed, part_grad, preferred_element_type=jn...  24 us
  transfers between devices with their start and end apart: 13, of which 7 were waited for; matrix products, arithmetic and copies ran while one was open for 10% of the time, Pallas kernels for 0%

profile of v1, /device:TPU:27, one launch (start us, length us, event | category | flops | bytes accessed | tf_op | source)
XLA Modules:
  0.0 682.1 jit_solution(7177296306694222611)
XLA Ops:
  15.2 3.1 dynamic-slice_bitcast_fusion.4
  18.4 2.3 copy-done.2
  21.6 2.3 collective-permute-start.6
  25.8 2.4 bitcast_dynamic-update-slice_fusion.7
  33.7 12.7 %collective-permute-done.1 = bf16[2,1,128,2048]{3,2,0,1:T(8,128)(2,1)} collective-permute-done((bf16[2,1,128,2048]{3,2,0,1:T(8,128)(2,1)}, bf16[2,1,128,2048]{3,2,0,1:T(8,128)(2,1)}, u32[]{:S(2)}, u32[]{:S(2)}) %collective-permute-start.1) | collective-permute-done | bytes 1048608 | tf_op jit(solution)/shard_map/ppermute | solution.py:37
  46.4 2.5 collective-permute-start.4
  51.2 63.1 %collective-permute-done.2 = bf16[2,1,128,2048]{3,2,0,1:T(8,128)(2,1)} collective-permute-done((bf16[2,1,128,2048]{3,2,0,1:T(8,128)(2,1)}, bf16[2,1,128,2048]{3,2,0,1:T(8,128)(2,1)}, u32[]{:S(2)}, u32[]{:S(2)}) %collective-permute-start.2) | collective-permute-done | bytes 1048608 | tf_op jit(solution)/shard_map/ppermute | solution.py:37
  114.2 2.3 bitcast_dynamic-update-slice_fusion.4
  117.7 5.0 collective-permute-done.4
  128.3 8.1 %gather_fusion = bf16[8,2,128,2048]{3,2,1,0:T(8,128)(2,1)} fusion(bf16[8,2,128,2048]{3,2,1,0:T(8,128)(2,1)} %bitcast.164, s32[1024]{0:T(1024)S(1)} %pad_clamp_fusion), kind=kCustom, calls=%fused_computation | custom fusion | bytes 16777248 | tf_op jit(solution)/shard_map/gather | solution.py:40
  136.3 8.4 %copy.56 = bf16[2,8,1,128,2048]{4,3,1,0,2:T(8,128)(2,1)} copy(bf16[2,8,1,128,2048]{4,3,0,1,2:T(8,128)(2,1)} %bitcast.162) | data formatting | bytes 16777216 | tf_op jit(solution)/shard_map/transpose | solution.py:25
  144.8 10.2 %fusion.17 = f32[2,2,384,1024]{2,3,1,0:T(8,128)S(1)} fusion(bf16[2,1024,2048,1]{2,1,3,0:T(8,128)(2,1)} %bitcast.165, bf16[2,2,384,2048]{3,2,1,0:T(8,128)(2,1)} %param.9), kind=kOutput, calls=%fused_computation.41 | convolution fusion | flops 6442450944 | bytes 20971520 | tf_op jit(solution)/shard_map/cefd,esd->ecfs/dot_general | solution.py:142
  157.7 9.1 %bitcast_convert_fusion = bf16[2,1024,2048]{2,1,0:T(8,128)(2,1)} fusion(bf16[2,2,384,2048]{3,2,1,0:T(8,128)(2,1)S(1)} %bitcast.172, bf16[2,1,384,1024]{2,3,1,0:T(8,128)(2,1)S(1)} %get-tuple-element.44, bf16[2,1,384,1024]{2,3,1,0:T(8,128)(2,1)S(1)} %get-tuple-element.43), kind=kOutput, calls=%fused_computation.1 | convolution fusion | flops 6448218112 | bytes 17825792 | tf_op jit(solution)/shard_map/ecfs,cefd->esd/dot_general | solution.py:151
  168.3 9.6 %convolution_bitcast_fusion = f32[1,2,384,2048]{3,2,1,0:T(8,128)} fusion(bf16[2,1024,2048]{2,1,0:T(8,128)(2,1)} %bitcast.166, s32[]{:T(128)S(6)} %select_n.146, bf16[2,1,384,1024]{2,3,1,0:T(8,128)(2,1)S(1)} %copy-done.8, bf16[2,1,384,1024]{2,3,1,0:T(8,128)(2,1)} %copy-done.9), kind=kOutput, calls=%fused_computation.22 | convolution fusion | flops 3222011904 | bytes 17825796 | tf_op jit(solution)/shard_map/esd,ecfs->cefd/dot_general | solution.py:166
  181.6 320.7 %all-reduce.3.cloned.1.call-done = bf16[2,8,2,64,2048]{4,3,2,1,0:T(8,128)(2,1)} async-done(((bf16[2,8,2,64,2048]{4,3,2,1,0:T(8,128)(2,1)}), bf16[2,8,2,64,2048]{4,3,2,1,0:T(8,128)(2,1)}) %all-reduce.3.cloned.1.call-update) | async-done | bytes 8388624
  502.3 3.1 dynamic-slice_bitcast_fusion
  507.7 5.5 all-to-all-start
  513.2 14.4 %fusion.7 = (bf16[1,2,384,2048]{3,2,1,0:T(8,128)(2,1)S(1)}, bf16[1,2,384,2048]{3,2,1,0:T(8,128)(2,1)S(1)}, bf16[1,2,384,2048]{3,2,1,0:T(8,128)(2,1)}) fusion(bf16[1,2,384,2048]{3,2,1,0:T(8,128)(2,1)} %param.11, bf16[1,2,384,2048]{3,2,1,0:T(8,128)(2,1)} %param.10, bf16[2,2,384,2048]{3,2,1,0:T(8,128)(2,1)} %param.9, s32[]{:T(128)S(6)} %select_n.145, ...), kind=kOutput, calls=%fused_computation.24 | convolution fusion | flops 3250323456 | bytes 36701184 | tf_op jit(solution)/shard_map/esd,ecfs->cefd/dot_general | solution.py:166
  538.7 3.7 fusion.13
  544.1 50.4 %collective-permute-done.9 = bf16[1,384,2048]{2,1,0:T(8,128)(2,1)} collective-permute-done((bf16[1,384,2048]{2,1,0:T(8,128)(2,1)}, bf16[1,384,2048]{2,1,0:T(8,128)(2,1)}, u32[]{:S(2)}, u32[]{:S(2)}) %collective-permute-start.9) | collective-permute-done | bytes 1572896 | tf_op jit(solution)/shard_map/ppermute | solution.py:49
  594.5 33.7 %collective-permute-done.8 = bf16[1,384,2048]{2,1,0:T(8,128)(2,1)} collective-permute-done((bf16[1,384,2048]{2,1,0:T(8,128)(2,1)}, bf16[1,384,2048]{2,1,0:T(8,128)(2,1)}, u32[]{:S(2)}, u32[]{:S(2)}) %collective-permute-start.8) | collective-permute-done | bytes 1572896 | tf_op jit(solution)/shard_map/ppermute | solution.py:49
  628.2 33.7 %collective-permute-done.10 = bf16[1,384,2048]{2,1,0:T(8,128)(2,1)} collective-permute-done((bf16[1,384,2048]{2,1,0:T(8,128)(2,1)}, bf16[1,384,2048]{2,1,0:T(8,128)(2,1)}, u32[]{:S(2)}, u32[]{:S(2)}) %collective-permute-start.10) | collective-permute-done | bytes 1572896 | tf_op jit(solution)/shard_map/ppermute | solution.py:49
  661.9 9.1 %broadcast_select_fusion = (bf16[1,2,384,2048]{3,2,1,0:T(8,128)(2,1)}, bf16[1,2,384,2048]{3,2,1,0:T(8,128)(2,1)}, bf16[1,2,384,2048]{3,2,1,0:T(8,128)(2,1)}) fusion(bf16[1,2,384,2048]{3,2,1,0:T(8,128)(2,1)} %copy-done.4, pred[2]{0:T(512)(128)(4,1)S(1)} %compare_and_fusion, bf16[384,2048]{1,0:T(8,128)(2,1)} %bitcast.45, ...), kind=kLoop, calls=%fused_computation.38 | loop fusion | flops 4718592 | bytes 23592962 | tf_op jit(solution)/shard_map/jit(_where)/select_n | solution.py:96
  671.1 2.6 copy.62
  (83 shorter events, 47.7 us)
Async XLA Ops:
  7.2 5.7 copy-start
  7.2 495.1 %all-reduce.3.cloned.1.call-start = ((), (), s32[]{:S(2)}) async-start(), calls=%async_computation.1 | async-start | bytes 16777216
  15.2 5.5 copy-start.2
  20.7 9.3 %collective-permute-start = (bf16[2,1,128,2048]{3,2,0,1:T(8,128)(2,1)}, bf16[2,1,128,2048]{3,2,0,1:T(8,128)(2,1)}, u32[]{:S(2)}, u32[]{:S(2)}) collective-permute-start(bf16[2,1,128,2048]{3,2,0,1:T(8,128)(2,1)} %get-tuple-element.42), channel_id=1, source_target_pairs={{0,2},{2,0},{4,6},{6,4},{8,10},{10,8},{12,14},{14,12},{1,3},{3,1},... | collective-permute-start | bytes 3145736 | tf_op jit(solution)/shard_map/ppermute | solution.py:37
  21.4 25.0 %collective-permute-start.1 = (bf16[2,1,128,2048]{3,2,0,1:T(8,128)(2,1)}, bf16[2,1,128,2048]{3,2,0,1:T(8,128)(2,1)}, u32[]{:S(2)}, u32[]{:S(2)}) collective-permute-start(bf16[2,1,128,2048]{3,2,0,1:T(8,128)(2,1)} %get-tuple-element.41), channel_id=1, source_target_pairs={{0,4},{2,6},{4,0},{6,2},{8,12},{10,14},{12,8},{14,10},{1,5},{3,7},... | collective-permute-start | bytes 3145736 | tf_op jit(solution)/shard_map/ppermute | solution.py:37
  21.6 104.3 %collective-permute-start.6 = (bf16[2,1,128,2048]{3,2,0,1:T(8,128)(2,1)}, bf16[2,1,128,2048]{3,2,0,1:T(8,128)(2,1)}, u32[]{:S(2)}, u32[]{:S(2)}) collective-permute-start(bf16[2,1,128,2048]{3,2,0,1:T(8,128)(2,1)} %get-tuple-element.36), channel_id=1, source_target_pairs={{0,14},{2,12},{4,10},{6,8},{8,6},{10,4},{12,2},{14,0},{1,15},{3,13... | collective-permute-start | bytes 3145736 | tf_op jit(solution)/shard_map/ppermute | solution.py:37
  24.0 99.7 %collective-permute-start.5 = (bf16[2,1,128,2048]{3,2,0,1:T(8,128)(2,1)}, bf16[2,1,128,2048]{3,2,0,1:T(8,128)(2,1)}, u32[]{:S(2)}, u32[]{:S(2)}) collective-permute-start(bf16[2,1,128,2048]{3,2,0,1:T(8,128)(2,1)} %get-tuple-element.37), channel_id=1, source_target_pairs={{0,12},{2,14},{4,8},{6,10},{8,4},{10,6},{12,0},{14,2},{1,13},{3,15... | collective-permute-start | bytes 3145736 | tf_op jit(solution)/shard_map/ppermute | solution.py:37
  24.1 90.1 %collective-permute-start.2 = (bf16[2,1,128,2048]{3,2,0,1:T(8,128)(2,1)}, bf16[2,1,128,2048]{3,2,0,1:T(8,128)(2,1)}, u32[]{:S(2)}, u32[]{:S(2)}) collective-permute-start(bf16[2,1,128,2048]{3,2,0,1:T(8,128)(2,1)} %get-tuple-element.40), channel_id=1, source_target_pairs={{0,6},{2,4},{4,2},{6,0},{8,14},{10,12},{12,10},{14,8},{1,7},{3,5},... | collective-permute-start | bytes 3145736 | tf_op jit(solution)/shard_map/ppermute | solution.py:37
  30.0 86.5 %collective-permute-start.3 = (bf16[2,1,128,2048]{3,2,0,1:T(8,128)(2,1)}, bf16[2,1,128,2048]{3,2,0,1:T(8,128)(2,1)S(1)}, u32[]{:S(2)}, u32[]{:S(2)}) collective-permute-start(bf16[2,1,128,2048]{3,2,0,1:T(8,128)(2,1)} %get-tuple-element.39), channel_id=1, source_target_pairs={{0,8},{2,10},{4,12},{6,14},{8,0},{10,2},{12,4},{14,6},{1,9},{3,11}... | collective-permute-start | bytes 3145736 | tf_op jit(solution)/shard_map/ppermute | solution.py:37
  46.4 76.2 %collective-permute-start.4 = (bf16[2,1,128,2048]{3,2,0,1:T(8,128)(2,1)}, bf16[2,1,128,2048]{3,2,0,1:T(8,128)(2,1)S(1)}, u32[]{:S(2)}, u32[]{:S(2)}) collective-permute-start(bf16[2,1,128,2048]{3,2,0,1:T(8,128)(2,1)} %get-tuple-element.38), channel_id=1, source_target_pairs={{0,10},{2,8},{4,14},{6,12},{8,2},{10,0},{12,6},{14,4},{1,11},{3,9}... | collective-permute-start | bytes 3145736 | tf_op jit(solution)/shard_map/ppermute | solution.py:37
  136.3 21.4 %slice-start = ((s8[6291456]{0:T(1024)(128)(4,1)}), s8[2097152]{0:T(1024)(128)(4,1)S(1)}, s32[]{:S(2)}) async-start(s8[6291456]{0:T(1024)(128)(4,1)} %bitcast.171), calls=%async_computation.2 | async-start | bytes 4194304
  144.8 12.9 %slice-start.1 = ((s8[6291456]{0:T(1024)(128)(4,1)}), s8[4194304]{0:T(1024)(128)(4,1)S(1)}, s32[]{:S(2)}) async-start(s8[6291456]{0:T(1024)(128)(4,1)} %bitcast.171), calls=%async_computation.3 | async-start | bytes 8388608
  157.7 9.2 %copy-start.7 = (bf16[2,1,384,1024]{2,3,1,0:T(8,128)(2,1)}, bf16[2,1,384,1024]{2,3,1,0:T(8,128)(2,1)S(1)}, u32[]{:S(2)}) copy-start(bf16[2,1,384,1024]{2,3,1,0:T(8,128)(2,1)S(1)} %get-tuple-element.43) | copy-start | bytes 4718596
  157.7 9.2 %copy-start.9 = (bf16[2,1,384,1024]{2,3,1,0:T(8,128)(2,1)}, bf16[2,1,384,1024]{2,3,1,0:T(8,128)(2,1)S(1)}, u32[]{:S(2)}) copy-start(bf16[2,1,384,1024]{2,3,1,0:T(8,128)(2,1)S(1)} %get-tuple-element.44) | copy-start | bytes 4718596
  168.3 10.2 %copy-start.10 = (s32[4,2]{0,1:T(2,128)S(1)}, s32[4,2]{0,1:T(2,128)}, u32[]{:S(2)}) copy-start(s32[4,2]{0,1:T(2,128)} %param.13) | copy-start | bytes 100
  168.3 12.1 %copy-start.11 = (u32[32]{0:T(128)S(1)}, u32[32]{0:T(128)}, u32[]{:S(2)}) copy-start(u32[32]{0:T(128)} %constant.183) | copy-start | bytes 388
  177.9 335.3 %collective-permute-start.7 = (f32[1,2,384,2048]{3,2,1,0:T(8,128)}, f32[1,2,384,2048]{3,2,1,0:T(8,128)}, u32[]{:S(2)}, u32[]{:S(2)}) collective-permute-start(f32[1,2,384,2048]{3,2,1,0:T(8,128)} %convolution_bitcast_fusion), channel_id=1, source_target_pairs={{0,16},{16,0},{1,17},{17,1},{2,18},{18,2},{3,19},{19,3},{4,20},{20... | collective-permute-start | bytes 18874376 | tf_op jit(solution)/shard_map/ppermute | solution.py:49
  507.7 163.4 %all-to-all-start = ((bf16[2,8,64,2048]{3,2,0,1:T(8,128)(2,1)}), bf16[2,8,64,2048]{3,2,0,1:T(8,128)(2,1)}, u32[]{:S(2)}, u32[]{:S(2)}) async-start(bf16[2,8,64,2048]{3,2,0,1:T(8,128)(2,1)} %copy.61), calls=%async_computation | async-start | bytes 8388608 | tf_op jit(solution)/shard_map/all_to_all | solution.py:157
  527.6 4.2 copy-start.5
  527.6 4.2 copy-start.6
  533.0 61.5 %collective-permute-start.9 = (bf16[1,384,2048]{2,1,0:T(8,128)(2,1)}, bf16[1,384,2048]{2,1,0:T(8,128)(2,1)}, u32[]{:S(2)}, u32[]{:S(2)}) collective-permute-start(bf16[1,384,2048]{2,1,0:T(8,128)(2,1)} %dynamic-slice_bitcast_fusion.2), channel_id=1, source_target_pairs={{0,8},{2,10},{4,12},{6,14},{8,0},{10,2},{12,4},{14,6},{1,9},{3,11}... | collective-permute-start | bytes 4718600 | tf_op jit(solution)/shard_map/ppermute | solution.py:49
  534.3 94.0 %collective-permute-start.8 = (bf16[1,384,2048]{2,1,0:T(8,128)(2,1)}, bf16[1,384,2048]{2,1,0:T(8,128)(2,1)}, u32[]{:S(2)}, u32[]{:S(2)}) collective-permute-start(bf16[1,384,2048]{2,1,0:T(8,128)(2,1)} %dynamic-slice_bitcast_fusion.3), channel_id=1, source_target_pairs={{0,8},{2,10},{4,12},{6,14},{8,0},{10,2},{12,4},{14,6},{1,9},{3,11}... | collective-permute-start | bytes 4718600 | tf_op jit(solution)/shard_map/ppermute | solution.py:49
  534.5 127.4 %collective-permute-start.10 = (bf16[1,384,2048]{2,1,0:T(8,128)(2,1)}, bf16[1,384,2048]{2,1,0:T(8,128)(2,1)}, u32[]{:S(2)}, u32[]{:S(2)}) collective-permute-start(bf16[1,384,2048]{2,1,0:T(8,128)(2,1)} %dynamic-slice_bitcast_fusion.1), channel_id=1, source_target_pairs={{0,8},{2,10},{4,12},{6,14},{8,0},{10,2},{12,4},{14,6},{1,9},{3,11}... | collective-permute-start | bytes 4718600 | tf_op jit(solution)/shard_map/ppermute | solution.py:49
  671.1 4.2 copy-start.1
  (3 other events, 7.2 us)
Sparse Core Ops, SparseCore 0:
  167.0 335.2 all-reduce.2
